TPU v7x, 512 devices: a whole 4x4x16 slice. The times are simulated.
512 devices in a mesh: seq: 128 (over y, z, core), tp: 4 (over x).
Axes of the slice: x: 4, y: 4, z: 16, core: 2. Of those that a mesh axis runs over, the one named last changes fastest.
Arguments:
- queries: float32 [16384, 2048], P('seq', 'tp'), may hold values from -6 to 6
- keys: float32 [16384, 2048], P('seq', 'tp'), may hold values from -6 to 6
- values: float32 [16384, 2048], P('seq', 'tp'), may hold values from -6 to 6
- out_weight: float32 [2048, 4096], P('seq', 'tp'), may hold values from -0.125 to 0.125
Outputs:
- mixed: float32 [16384, 4096], P('seq', 'tp')
All inputs are finite; a program needn't handle non-finite values.
Results may differ from a plain program's by a relative error of at most 0.0003.
Values sent between devices are 32-bit elements; how exact they have to be, the bound alone decides.
A program may use at most 128 MiB of HBM per device.

v0:
```python
import jax
import jax.numpy as jnp
from jax import lax
from jax.sharding import PartitionSpec as P

DH = 128


def prefix(part, axis, combine, identity):
    place = lax.axis_index(axis)
    gathered = jax.tree.map(lambda a: lax.all_gather(a, axis), part)
    state = jax.tree.map(lambda a, e: jnp.zeros_like(a) + jnp.asarray(e, a.dtype), part, identity)

    def one(step, state):
        return combine(
            state, jax.tree.map(lambda a: lax.dynamic_index_in_dim(a, step, 0, False), gathered)
        )

    return lax.fori_loop(0, place, one, state)


def features(inputs):
    return jnp.where(inputs > 0, inputs + 1.0, jnp.exp(jnp.minimum(inputs, 0.0)))


def combine(earlier, later):
    return (earlier[0] + later[0], earlier[1] + later[1])


def shards(queries, keys, values, out_weight):
    highest = lax.Precision.HIGHEST
    tok_rows = queries.shape[0]
    heads_here = queries.shape[1] // DH
    phi_queries = features(queries).reshape(tok_rows, heads_here, DH)
    phi_keys = features(keys).reshape(tok_rows, heads_here, DH)
    value_heads = values.reshape(tok_rows, heads_here, DH)
    memory_state = jnp.einsum("shd,she->hde", phi_keys, value_heads, precision=highest)
    key_total = jnp.sum(phi_keys, axis=0)
    identity = (jnp.zeros_like(memory_state), jnp.zeros_like(key_total))
    prior_state, prior_total = prefix((memory_state, key_total), "seq", combine, identity)
    causal_mask = jnp.arange(tok_rows)[:, None] >= jnp.arange(tok_rows)[None, :]
    scores = jnp.einsum("thd,shd->hts", phi_queries, phi_keys, precision=highest)
    scores = jnp.where(causal_mask[None], scores, 0.0)
    numerator = jnp.einsum("hts,shd->thd", scores, value_heads, precision=highest)
    numerator = numerator + jnp.einsum("thd,hde->the", phi_queries, prior_state, precision=highest)
    denominator = jnp.sum(scores, axis=2).T + jnp.einsum(
        "thd,hd->th", phi_queries, prior_total, precision=highest
    )
    attended = (numerator / denominator[:, :, None]).reshape(tok_rows, heads_here * DH)
    every_head = lax.all_gather(attended, "tp", axis=1, tiled=True)
    gathered = lax.all_gather(out_weight, "seq", axis=0, tiled=True)
    mixed = jnp.dot(every_head, gathered, precision=highest, preferred_element_type=jnp.float32)
    return mixed


def solution(mesh):
    return jax.shard_map(
        shards,
        mesh=mesh,
        in_specs=(P("seq", "tp"), P("seq", "tp"), P("seq", "tp"), P("seq", "tp")),
        out_specs=P("seq", "tp"),
        check_vma=False,
    )
```

profile of v0, /device:TPU:1, one launch (start us, length us, event | category | flops | bytes accessed | tf_op | source)
XLA Modules:
  0.0 401.2 jit_solution(6245858117362999715)
XLA Ops:
  6.5 0.0 copy-start
  6.5 0.0 all-gather.9.cloned.1.call-start
  6.5 1.1 fusion.7
  7.6 0.1 copy.31
  7.7 0.0 copy-done
  7.8 1.1 fusion.3
  8.8 0.0 all-gather.9.cloned.1.call-update
  8.9 0.0 all-gather.7.cloned.1.call-start
  8.9 0.7 all-gather.7.cloned.1.call-update
  9.6 0.0 all-gather.5.cloned.1.call-start
  9.7 1.0 exponential_select_fusion.1
  10.7 0.1 copy.30
  10.8 108.5 %all_gather.21 = f32[128,4,128]{2,1,0:T(4,128)S(1)} all-gather(f32[1,4,128]{2,1,0:T(4,128)S(1)} %bitcast.58), channel_id=1, replica_groups=mesh['seq'=128,'tp'=4] {'seq'}, dimensions={0}, use_global_device_ids=true | all-gather | bytes 264192 | tf_op jit(solution)/shard_map/all_gather | solution.py:11
  119.4 0.6 fusion.8
  120.0 0.6 convolution_bitcast_fusion.1
  120.6 90.9 %all-gather.9.cloned.1.call-done = f32[512,128,128]{2,1,0:T(8,128)} async-done(((f32[4,128,128]{2,1,0:T(8,128)}), f32[512,128,128]{2,1,0:T(8,128)}) %all-gather.9.cloned.1.call-update) | async-done | bytes 33554448 | tf_op jit(solution)/shard_map/all_gather | solution.py:11
  211.6 1.1 while.12
  211.6 1.0 bitcast_add_fusion.4
  212.6 0.3 fusion.9
  212.9 1.3 fusion.1
  214.3 0.0 all-gather.5.cloned.1.call-update
  214.3 143.7 %all-gather.7.cloned.1.call-done = f32[2048,1024]{1,0:T(8,128)} async-done(((f32[16,1024]{1,0:T(8,128)}), f32[2048,1024]{1,0:T(8,128)}) %all-gather.7.cloned.1.call-update) | async-done | bytes 8388624 | tf_op jit(solution)/shard_map/all_gather | solution.py:51
  358.0 27.5 %all-gather.5.cloned.1.call-done = f32[128,2048]{0,1:T(8,128)} async-done(((f32[128,512]{0,1:T(8,128)}), f32[128,2048]{0,1:T(8,128)}) %all-gather.5.cloned.1.call-update) | async-done | bytes 1048592 | tf_op jit(solution)/shard_map/all_gather | solution.py:50
  385.5 9.1 %fusion.10 = f32[128,1024]{1,0:T(8,128)} fusion(f32[128,2048]{0,1:T(8,128)} %all-gather.5.cloned.1.call-done, f32[2048,1024]{1,0:T(8,128)} %all-gather.7.cloned.1.call-done), kind=kOutput, calls=%fused_computation.19 | convolution fusion | flops 3221225472 | bytes 9961472 | tf_op jit(solution)/shard_map/dot_general | solution.py:52
  (5 shorter events, 0.1 us)
Async XLA Ops:
  6.5 1.2 copy-start
  6.5 205.0 %all-gather.9.cloned.1.call-start = ((), (), s32[]{:S(2)}) async-start(), calls=%async_computation.2 | async-start | bytes 33816576 | tf_op jit(solution)/shard_map/all_gather | solution.py:11
  8.9 349.1 %all-gather.7.cloned.1.call-start = ((), (), s32[]{:S(2)}) async-start(), calls=%async_computation.1 | async-start | bytes 8454144 | tf_op jit(solution)/shard_map/all_gather | solution.py:51
  9.6 375.9 %all-gather.5.cloned.1.call-start = ((), (), s32[]{:S(2)}) async-start(), calls=%async_computation | async-start | bytes 1310720 | tf_op jit(solution)/shard_map/all_gather | solution.py:50
Sparse Core Ops, SparseCore 0:
  10.5 200.9 all-gather.8
  214.7 143.2 all-gather.6
  360.1 25.3 all-gather.4
where the time goes:
time: 405 us; the launch traced here: 401 us
  waiting for transfers between devices  263 us (65%)
  blocking collectives  109 us (27%)
  between operations  13.2 us (3%)
  matrix products  13.1 us (3%)
    all_gather x1, waiting for transfers between devices, shards(): gathered = lax.all_gather(out_weight, 'seq', axis=0, tiled=True)  144 us
    all_gather x1, blocking collectives, prefix(): gathered = jax.tree.map(lambda a: lax.all_gather(a, axis), part)  109 us
    all_gather x1, waiting for transfers between devices, prefix(): gathered = jax.tree.map(lambda a: lax.all_gather(a, axis), part)  90.9 us
    all_gather x1, waiting for transfers between devices, shards(): every_head = lax.all_gather(attended, 'tp', axis=1, tiled=True)  27.5 us
    dot_general x1, matrix products, shards(): jnp.dot(every_head, gathered, precision=highest, preferred_element_type=j...  9.14 us
  transfers between devices with their start and end apart: 3, of which 3 were waited for; matrix products, arithmetic and copies ran while one was open for 1% of the time, Pallas kernels for 0%

commit v1 on v0

--- a/solution.py
+++ b/solution.py
@@ -47,7 +47,14 @@
         "thd,hd->th", phi_queries, prior_total, precision=highest
     )
     attended = (numerator / denominator[:, :, None]).reshape(tok_rows, heads_here * DH)
-    every_head = lax.all_gather(attended, "tp", axis=1, tiled=True)
+    n_parts = lax.axis_size("tp")
+    items = tuple(((pp, (pp + 1) % n_parts) for pp in range(n_parts)))
+    then = [None] * n_parts
+    then[n_parts - 1] = attended
+    for dev_i in range(n_parts - 2, -1, -1):
+        then[dev_i] = lax.ppermute(then[dev_i + 1], axis_name="tp", perm=items)
+    arr_out = jnp.concatenate(then, 1)
+    every_head = jnp.roll(arr_out, (lax.axis_index("tp") + 1) * attended.shape[1], 1)
     gathered = lax.all_gather(out_weight, "seq", axis=0, tiled=True)
     mixed = jnp.dot(every_head, gathered, precision=highest, preferred_element_type=jnp.float32)
     return mixed

time: 405 us -> 387 us (0.956)
  the two profiles are of different devices: /device:TPU:1 before, /device:TPU:504 now
where the time goes in v1:
time: 387 us; the launch traced here: 383 us
  other arithmetic  131 us (34%)
  waiting for transfers between devices  118 us (30%)
  blocking collectives  98 us (25%)
  between operations  13.6 us (4%)
  matrix products  11 us (3%)
  starting transfers between devices  7.5 us (2%)
    add x252, other arithmetic, combine(): return (earlier[0] + later[0], earlier[1] + later[1])  130 us
    all_gather x1, blocking collectives, prefix(): gathered = jax.tree.map(lambda a: lax.all_gather(a, axis), part)  98 us
    all_gather x1, waiting for transfers between devices, prefix(): gathered = jax.tree.map(lambda a: lax.all_gather(a, axis), part)  90.8 us
    ppermute x3, waiting for transfers between devices, shards(): then[dev_i] = lax.ppermute(then[dev_i + 1], axis_name='tp', perm=items)  26.5 us
    dot_general x1, matrix products, shards(): jnp.dot(every_head, gathered, precision=highest, preferred_element_type=j...  7.79 us
  transfers between devices with their start and end apart: 5, of which 4 were waited for; matrix products, arithmetic and copies ran while one was open for 34% of the time, Pallas kernels for 0%

profile of v1, /device:TPU:504, one launch (start us, length us, event | category | flops | bytes accessed | tf_op | source)
XLA Modules:
  0.0 383.0 jit_solution(5748981289332566701)
XLA Ops:
  6.5 1.1 fusion.10
  7.8 1.1 fusion.5
  9.9 98.0 %all_gather.18 = f32[128,4,128]{2,1,0:T(4,128)S(1)} all-gather(f32[1,4,128]{2,1,0:T(4,128)S(1)} %bitcast.59), channel_id=1, replica_groups=mesh['seq'=128,'tp'=4] {'seq'}, dimensions={0}, use_global_device_ids=true | all-gather | bytes 264192 | tf_op jit(solution)/shard_map/all_gather | solution.py:11
  109.0 90.8 %all-gather.6.cloned.1.call-done = f32[512,128,128]{2,1,0:T(8,128)} async-done(((f32[4,128,128]{2,1,0:T(8,128)}), f32[512,128,128]{2,1,0:T(8,128)}) %all-gather.6.cloned.1.call-update) | async-done | bytes 33554448 | tf_op jit(solution)/shard_map/all_gather | solution.py:11
  199.8 133.4 %while.12 = (s32[]{:T(128)}, f32[4,128,128]{2,1,0:T(8,128)S(1)}, f32[4,128]{1,0:T(4,128)S(1)}, s32[]{:T(128)}, f32[128,4,128,128]{3,2,1,0:T(8,128)}, /*index=5*/...) while((s32[]{:T(128)}, f32[4,128,128]{2,1,0:T(8,128)S(1)}, f32[4,128]{1,0:T(4,128)S(1)}, s32[]{:T(128)}, ...), condition=%wide.region_2.3_spmd, body=%wide.region_1.2_spmd.sunk | while | flops 66053 | bytes 792711 | solution.py:19
  234.8 1.0 bitcast_add_fusion.4
  292.9 1.0 bitcast_add_fusion.4
  296.1 1.0 bitcast_add_fusion.4
  297.2 1.0 bitcast_add_fusion.4
  302.5 1.0 bitcast_add_fusion.4
  304.6 1.0 bitcast_add_fusion.4
  308.8 1.0 bitcast_add_fusion.4
  309.9 1.0 bitcast_add_fusion.4
  311.0 1.0 bitcast_add_fusion.4
  314.1 1.0 bitcast_add_fusion.4
  316.3 1.0 bitcast_add_fusion.4
  323.7 1.0 bitcast_add_fusion.4
  334.1 3.4 collective-permute-start
  337.5 8.6 %collective-permute-done = f32[128,512]{0,1:T(8,128)S(1)} collective-permute-done((f32[128,512]{0,1:T(8,128)S(1)}, f32[128,512]{0,1:T(8,128)S(1)}, u32[]{:S(2)}, u32[]{:S(2)}) %collective-permute-start) | collective-permute-done | bytes 262176 | tf_op jit(solution)/shard_map/ppermute | solution.py:55
  346.1 2.2 collective-permute-start.1
  348.3 9.3 %collective-permute-done.1 = f32[128,512]{0,1:T(8,128)S(1)} collective-permute-done((f32[128,512]{0,1:T(8,128)S(1)}, f32[128,512]{0,1:T(8,128)S(1)}, u32[]{:S(2)}, u32[]{:S(2)}) %collective-permute-start.1) | collective-permute-done | bytes 262176 | tf_op jit(solution)/shard_map/ppermute | solution.py:55
  357.6 1.9 collective-permute-start.2
  359.5 8.7 %collective-permute-done.2 = f32[128,512]{0,1:T(8,128)S(1)} collective-permute-done((f32[128,512]{0,1:T(8,128)S(1)}, f32[128,512]{0,1:T(8,128)S(1)}, u32[]{:S(2)}, u32[]{:S(2)}) %collective-permute-start.2) | collective-permute-done | bytes 262176 | tf_op jit(solution)/shard_map/ppermute | solution.py:55
  368.4 7.8 %fusion.2 = f32[128,1024]{1,0:T(8,128)} fusion(f32[2048,1024]{1,0:T(8,128)} %all-gather.4.cloned.1.call-done, f32[128,4096]{0,1:T(8,128)S(1)} %constant_dynamic-update-slice_fusion, s32[]{:T(128)S(6)} %select_n.34), kind=kOutput, calls=%fused_computation.7 | convolution fusion | flops 3221225472 | bytes 9961476 | tf_op jit(solution)/shard_map/dot_general | solution.py:59
  (268 shorter events, 120.7 us)
Async XLA Ops:
  6.5 1.2 copy-start
  6.5 3.1 copy-start.1
  6.5 193.3 %all-gather.6.cloned.1.call-start = ((), (), s32[]{:S(2)}) async-start(), calls=%async_computation.1 | async-start | bytes 33816576 | tf_op jit(solution)/shard_map/all_gather | solution.py:11
  8.9 359.5 %all-gather.4.cloned.1.call-start = ((), (), s32[]{:S(2)}) async-start(), calls=%async_computation | async-start | bytes 8454144 | tf_op jit(solution)/shard_map/all_gather | solution.py:58
  334.1 12.0 %collective-permute-start = (f32[128,512]{0,1:T(8,128)S(1)}, f32[128,512]{0,1:T(8,128)S(1)}, u32[]{:S(2)}, u32[]{:S(2)}) collective-permute-start(f32[128,512]{0,1:T(8,128)S(1)} %bitcast.54), channel_id=1, source_target_pairs={{0,1},{1,2},{2,3},{3,0},{4,5},{5,6},{6,7},{7,4},{8,9},{9,10},{10,1... | collective-permute-start | bytes 786440 | tf_op jit(solution)/shard_map/ppermute | solution.py:55
  346.1 11.4 %collective-permute-start.1 = (f32[128,512]{0,1:T(8,128)S(1)}, f32[128,512]{0,1:T(8,128)S(1)}, u32[]{:S(2)}, u32[]{:S(2)}) collective-permute-start(f32[128,512]{0,1:T(8,128)S(1)} %collective-permute-done), channel_id=1, source_target_pairs={{0,1},{1,2},{2,3},{3,0},{4,5},{5,6},{6,7},{7,4},{8,9},{9,10},{10,1... | collective-permute-start | bytes 786440 | tf_op jit(solution)/shard_map/ppermute | solution.py:55
  357.6 10.6 %collective-permute-start.2 = (f32[128,512]{0,1:T(8,128)S(1)}, f32[128,512]{0,1:T(8,128)S(1)}, u32[]{:S(2)}, u32[]{:S(2)}) collective-permute-start(f32[128,512]{0,1:T(8,128)S(1)} %collective-permute-done.1), channel_id=1, source_target_pairs={{0,1},{1,2},{2,3},{3,0},{4,5},{5,6},{6,7},{7,4},{8,9},{9,10},{10,1... | collective-permute-start | bytes 786440 | tf_op jit(solution)/shard_map/ppermute | solution.py:55
Sparse Core Ops, SparseCore 0:
  10.5 189.2 all-gather.5
  202.9 144.4 all-gather.3
